TPU v7x, 32 devices: a whole 2x2x4 slice. The times are simulated.
32 devices in a mesh: gx: 4 (over x, core), gy: 8 (over z, y).
Axes of the slice: x: 2, y: 2, z: 4, core: 2. Of those that a mesh axis runs over, the one named last changes fastest.
Arguments:
- velocity: float32 [2, 11, 32, 1024], P(None, None, 'gx', 'gy'), may hold values from -6 to 6
- thickness: float32 [32, 1024], P('gx', 'gy'), may hold values from 0.5 to 2
- log_friction: float32 [32, 1024], P('gx', 'gy'), may hold values from -1 to 1
- obs_weight: float32 [32, 1024], P('gx', 'gy'), may hold values from 0.5 to 4
- ice_mask: int32 [32, 1024], P('gx', 'gy'), may hold values 0 or 1
- grounded: int32 [32, 1024], P('gx', 'gy'), may hold values 0 or 1
- probes: float32 [8, 32, 1024], P(None, 'gx', 'gy'), may hold values from -6 to 6
Outputs:
- hess_probe: float32 [8, 32, 1024], P(None, 'gx', 'gy')
All inputs are finite; a program needn't handle non-finite values. No bound on the sum of `ice_mask` or of `grounded` on one device may be relied on, other than what follows from the above.
Results may differ from a plain program's by a relative error of at most 0.0003.
Values sent between devices are 32-bit elements; how exact they have to be, the bound alone decides.
A program may use at most 64 MiB of HBM per device.

v0:
```python
import functools

import jax
import jax.numpy as jnp
from jax import lax
from jax.experimental import pallas as pl
from jax.experimental.pallas import tpu as pltpu
from jax.sharding import PartitionSpec as P

MASS_TERM = 0.1
STRAIN_OFFSET = 0.01
ANISO_X = (4.0, 1.0)
ANISO_Y = (1.0, 4.0)
HIGHEST = lax.Precision.HIGHEST
MESH = pl.DeviceIdType.MESH
PAIR = 2


def round_up(value, step):
    return (value + step - 1) // step * step


def kernel(
    sizes,
    vel_ref, thick_ref, logf_ref, obs_ref, ice_ref, ground_ref, probes_ref,
    out_ref,
    xs1, xr1, ys1, yr1,
    xs2, xr2, ys2, yr2,
    xs3, xr3, ys3, yr3,
    ys4, yr4, ub,
    coef, kzs, ratio, inverse, green, weight, bext, bedge, uedge,
    fields, tile_src, ar_x, ar_y,
    send_sem, recv_sem, axs, axr, ays, ayr,
):
    n_gx, n_gy = sizes
    layers = vel_ref.shape[1]
    rows = vel_ref.shape[2]
    lanes = vel_ref.shape[3]
    probes = probes_ref.shape[0]
    half = probes // 2
    comps = 2 * layers
    last = layers - 1
    ix = lax.axis_index("gx")
    iy = lax.axis_index("gy")
    tile = (rows, lanes)
    lane = lax.broadcasted_iota(jnp.int32, tile, 1)
    sub = lax.broadcasted_iota(jnp.int32, tile, 0)
    slot = ((lane + 1) >> 1) & (lanes // 2 - 1)
    even = (lane & 1) == 0
    lane_first = lane == 0
    lane_last = lane == lanes - 1
    sub_first = sub == 0
    sub_last = sub == rows - 1

    barrier = pltpu.get_barrier_semaphore()
    for step in range(1, n_gx):
        pl.semaphore_signal(barrier, inc=1, device_id={"gx": lax.rem(ix + step, n_gx)}, device_id_type=MESH)
    for step in range(1, n_gy):
        pl.semaphore_signal(barrier, inc=1, device_id={"gy": lax.rem(iy + step, n_gy)}, device_id_type=MESH)

    def transfer(phase, way, src, dst):
        axis, idx, count = ("gx", ix, n_gx) if way < 2 else ("gy", iy, n_gy)
        down = way % 2 == 0
        has_dst = idx > 0 if down else idx < count - 1
        has_src = idx < count - 1 if down else idx > 0
        copy = pltpu.make_async_remote_copy(
            src_ref=src, dst_ref=dst,
            send_sem=send_sem.at[phase, way], recv_sem=recv_sem.at[phase, way],
            device_id={axis: idx - 1 if down else idx + 1}, device_id_type=MESH,
        )
        return copy, dst, has_dst, has_src

    def exchange(phase, x_src, x_dst, y_src, y_dst):
        return (
            transfer(phase, 0, x_src[0], x_dst[1]),
            transfer(phase, 1, x_src[1], x_dst[0]),
            transfer(phase, 2, y_src, y_dst[1]),
            transfer(phase, 3, y_src, y_dst[0]),
        )

    def clear(transfers):
        for _, dst, _, has_src in transfers:
            @pl.when(jnp.logical_not(has_src))
            def _(dst=dst):
                dst[...] = jnp.zeros(dst.shape, jnp.float32)

    def start(transfers):
        for copy, _, has_dst, _ in transfers:
            pl.when(has_dst)(copy.start)

    def finish(transfers):
        for copy, _, has_dst, has_src in transfers:
            pl.when(has_src)(copy.wait_recv)
        for copy, _, has_dst, has_src in transfers:
            pl.when(has_dst)(copy.wait_send)

    ex1 = exchange(0, (xs1.at[0], xs1.at[1]), (xr1.at[0], xr1.at[1]), ys1, (yr1.at[0], yr1.at[1]))
    ex2 = exchange(1, (xs2.at[0], xs2.at[1]), (xr2.at[0], xr2.at[1]), ys2, (yr2.at[0], yr2.at[1]))
    ex3 = exchange(2, (xs3.at[0], xs3.at[1]), (xr3.at[0], xr3.at[1]), ys3, (yr3.at[0], yr3.at[1]))
    ex45 = [
        exchange(
            3 + p,
            (ub.at[p, 1], ub.at[p, rows]), (ub.at[p, 0], ub.at[p, rows + 1]),
            ys4.at[p], (yr4.at[p, 0], yr4.at[p, 1]),
        )
        for p in range(2)
    ]

    def pack(tiles):
        packed = tiles[0]
        for m in range(1, len(tiles)):
            packed = jnp.where(slot == m, pltpu.roll(tiles[m], 2 * m, 1), packed)
        return packed

    def merge(south, north):
        return jnp.where(even, pltpu.roll(south, 1, 1), pltpu.roll(north, lanes - 1, 1))

    def unpack(merged, m):
        return merged if m == 0 else pltpu.roll(merged, lanes - 2 * m, 1)

    def west(t, row):
        return jnp.where(sub_first, row, pltpu.roll(t, 1, 0))

    def east(t, row):
        return jnp.where(sub_last, row, pltpu.roll(t, rows - 1, 0))

    def south(t, edge):
        return jnp.where(lane_first, edge, pltpu.roll(t, 1, 1))

    def north(t, edge):
        return jnp.where(lane_last, edge, pltpu.roll(t, lanes - 1, 1))

    def ahead(t, d):
        return t if d == 0 else pltpu.roll(t, probes - d, 0)

    mask = ice_ref[...].astype(jnp.float32)
    friction = mask * ground_ref[...].astype(jnp.float32) * jnp.exp(logf_ref[...])
    wm = obs_ref[...] * mask
    fields[0] = friction
    fields[1] = wm
    natural = [vel_ref[c, l] for c in range(2) for l in range(layers)] + [mask, wm]
    for k, t in enumerate(natural):
        xs1[0, k : k + 1, :] = t[0:1, :]
        xs1[1, k : k + 1, :] = t[rows - 1 : rows, :]
    base1 = round_up(len(natural), 8)
    drive = [friction * vel_ref[c, 0] for c in range(2)]
    for i in range(rows):
        probe = probes_ref[:, i, :]
        for c in range(2):
            bext[0, c, i + 1] = probe * drive[c][i : i + 1, :]
    for c in range(2):
        xs1[0, base1 + c * probes : base1 + (c + 1) * probes, :] = bext[0, c, 1]
        xs1[1, base1 + c * probes : base1 + (c + 1) * probes, :] = bext[0, c, rows]
    ys1[0:rows, :] = pack(natural)
    ys1[rows:, :] = pack([bext[0, c, i + 1] for c in range(2) for i in range(rows)])

    for ex in (ex1, ex2, ex3, ex45[0], ex45[1]):
        clear(ex)
    pl.semaphore_wait(barrier, n_gx + n_gy - 2)
    start(ex1)
    finish(ex1)

    merged1 = merge(yr1[0, 0:rows, :], yr1[1, 0:rows, :])
    edge1 = [unpack(merged1, k) for k in range(len(natural))]
    mergedb = merge(yr1[0, rows:, :], yr1[1, rows:, :])
    for c in range(2):
        bext[0, c, 0] = xr1[0, base1 + c * probes : base1 + (c + 1) * probes, :]
        bext[0, c, rows + 1] = xr1[1, base1 + c * probes : base1 + (c + 1) * probes, :]
        for i in range(rows):
            bedge[0, c, i] = unpack(mergedb, c * rows + i)

    def around(t, k):
        return (
            west(t, xr1[0, k : k + 1, :]), east(t, xr1[1, k : k + 1, :]),
            south(t, edge1[k]), north(t, edge1[k]),
        )

    inverse_step = last / thick_ref[...]
    half_step = 0.5 * inverse_step
    visc = []
    for l in range(layers):
        grads = []
        for c in range(2):
            w, e, s, n = around(vel_ref[c, l], c * layers + l)
            dz = (vel_ref[c, min(l + 1, last)] - vel_ref[c, max(l - 1, 0)]) * half_step
            grads.append((0.5 * (e - w), 0.5 * (n - s), dz))
        (ux, uy, uz), (vx, vy, vz) = grads
        shear = uy + vx
        strain = ux * ux + vy * vy + ux * vy + 0.25 * (shear * shear) + 0.25 * (uz * uz + vz * vz) + STRAIN_OFFSET
        root = jnp.exp(jnp.log(strain) * (-1.0 / 3.0))
        root = root + root * (1.0 - strain * root * root * root) * (1.0 / 3.0)
        mu = jnp.where(mask > 0.5, 0.5 * root, 0.0)
        visc.append(mu)
        xs2[0, l : l + 1, :] = mu[0:1, :]
        xs2[1, l : l + 1, :] = mu[rows - 1 : rows, :]
    ys2[...] = pack(visc)
    start(ex2)
    mask_w, mask_e, mask_s, mask_n = (0.5 * mask * m for m in around(mask, comps))
    step2 = inverse_step * inverse_step
    kz = [0.5 * (visc[l] + visc[l + 1]) * step2 for l in range(last)]
    for l in range(last):
        kzs[l] = kz[l]
    diag = MASS_TERM * mask + (1.0 - mask)
    finish(ex2)
    merged2 = merge(yr2[0], yr2[1])
    for l in range(layers):
        mu = visc[l]
        edge = unpack(merged2, l)
        coef[0, l] = (mu + west(mu, xr2[0, l : l + 1, :])) * mask_w
        coef[1, l] = (mu + east(mu, xr2[1, l : l + 1, :])) * mask_e
        coef[2, l] = (mu + south(mu, edge)) * mask_s
        coef[3, l] = (mu + north(mu, edge)) * mask_n

    for c in range(2):
        ratios, inverses = [], []
        for l in range(layers):
            pivot = ANISO_X[c] * (coef[0, l] + coef[1, l]) + ANISO_Y[c] * (coef[2, l] + coef[3, l]) + diag
            if l == 0:
                pivot = pivot + friction
            if l > 0:
                pivot = pivot + kz[l - 1]
            if l < last:
                pivot = pivot + kz[l]
            if l > 0:
                pivot = pivot - kz[l - 1] * ratios[-1]
            inv = 1.0 / pivot
            inverses.append(inv)
            inverse[c, l] = inv
            if l < last:
                ratios.append(kz[l] * inv)
                ratio[c, l] = ratios[-1]
        up = [inverses[0]]
        for l in range(1, layers):
            up.append(kz[l - 1] * up[-1] * inverses[l])
        low, top = up[last], inverses[last]
        for l in range(last, -1, -1):
            if l < last:
                low = up[l] + ratios[l] * low
                top = ratios[l] * top
            green[0, c, l] = low
            green[1, c, l] = top
    tiles3 = []
    for p in range(2):
        for c in range(2):
            for l in range(layers):
                k = len(tiles3)
                t = green[p, c, l]
                tiles3.append(t)
                xs3[0, k : k + 1, :] = t[0:1, :]
                xs3[1, k : k + 1, :] = t[rows - 1 : rows, :]
    ys3[...] = pack(tiles3)
    start(ex3)
    finish(ex3)
    merged3 = merge(yr3[0], yr3[1])
    for p in range(2):
        for c in range(2):
            for l in range(layers):
                k = (p * 2 + c) * layers + l
                t = green[p, c, l]
                edge = unpack(merged3, k)
                weight[p, c, 0, l] = ANISO_X[c] * coef[0, l] * west(t, xr3[0, k : k + 1, :])
                weight[p, c, 1, l] = ANISO_X[c] * coef[1, l] * east(t, xr3[1, k : k + 1, :])
                weight[p, c, 2, l] = ANISO_Y[c] * coef[2, l] * south(t, edge)
                weight[p, c, 3, l] = ANISO_Y[c] * coef[3, l] * north(t, edge)

    zero = jnp.zeros((probes, lanes), jnp.float32)

    def outer(acc, left, right):
        return tuple(acc[d] + left * ahead(right, d) for d in range(half + 1))

    def solve(p):
        src = 0 if p == 0 else last
        dst = last - src

        def first(t, accs):
            acc_s, acc_1, acc_2 = accs
            packed = None
            for ii in range(PAIR):
                i = t * PAIR + ii
                for c in range(2):
                    b0 = bext[p, c, i + 1]
                    bw = bext[p, c, i]
                    be = bext[p, c, i + 2]
                    edge = bedge[p, c, i]
                    bs = south(b0, edge)
                    bn = north(b0, edge)
                    lateral, y = [], []
                    for l in range(layers):
                        n1 = (
                            weight[p, c, 0, l, pl.ds(i, 1), :] * bw
                            + weight[p, c, 1, l, pl.ds(i, 1), :] * be
                            + weight[p, c, 2, l, pl.ds(i, 1), :] * bs
                            + weight[p, c, 3, l, pl.ds(i, 1), :] * bn
                        )
                        lateral.append(n1)
                        if l > 0:
                            n1 = n1 + kzs[l - 1, pl.ds(i, 1), :] * y[-1]
                        y.append(n1 * inverse[c, l, pl.ds(i, 1), :])
                    x = y[last]
                    for l in range(last, -1, -1):
                        if l < last:
                            x = y[l] + ratio[c, l, pl.ds(i, 1), :] * x
                        ub[p, i + 1, c * layers + l] = x
                        m = (ii * 2 + c) * layers + l
                        moved = x if m == 0 else pltpu.roll(x, 2 * m, 1)
                        packed = moved if packed is None else jnp.where(slot == m, moved, packed)
                        acc_2 = outer(acc_2, lateral[l], x)
                        if l == src:
                            acc_1 = outer(acc_1, b0, x)
                    acc_s = outer(acc_s, green[p, c, src, pl.ds(i, 1), :] * b0, b0)
            ys4[p, pl.ds(pl.multiple_of(t * rows, rows), rows), :] = packed
            return acc_s, acc_1, acc_2

        none = (zero,) * (half + 1)
        acc_s, acc_1, acc_2 = lax.fori_loop(0, rows // PAIR, first, (none, none, none))
        start(ex45[p])
        finish(ex45[p])

        def second(t, acc_3):
            at = pl.ds(pl.multiple_of(t * rows, rows), rows)
            merged = merge(yr4[p, 0, at, :], yr4[p, 1, at, :])
            for ii in range(PAIR):
                i = t * PAIR + ii
                for l in range(layers):
                    cw, ce, cs, cn = (coef[q, l, pl.ds(i, 1), :] for q in range(4))
                    for c in range(2):
                        k = c * layers + l
                        w0 = ub[p, i + 1, k]
                        edge = unpack(merged, ii * comps + k)
                        if l == dst:
                            uedge[c, i] = edge
                        n2 = ANISO_X[c] * (cw * ub[p, i, k] + ce * ub[p, i + 2, k]) + ANISO_Y[c] * (
                            cs * south(w0, edge) + cn * north(w0, edge)
                        )
                        acc_3 = outer(acc_3, n2, w0)
            return acc_3

        acc_3 = lax.fori_loop(0, rows // PAIR, second, none)

        grams = jnp.zeros((probes, lanes), jnp.float32)
        for g, acc in enumerate((acc_s, acc_1, acc_2, acc_3)):
            for d in range(half + 1):
                total = jnp.broadcast_to(jnp.sum(acc[d], axis=1, keepdims=True), (probes, lanes))
                grams = jnp.where(lane == g * probes + (sub + d) % probes, total, grams)
                if 0 < d < half:
                    moved = pltpu.roll(total, d, 0)
                    grams = jnp.where(lane == g * probes + (sub + probes - d) % probes, moved, grams)

        def reduce_axis(value, stage, axis, idx, count, landed, ssem, rsem):
            tile_src[p, stage] = value
            copies = [
                pltpu.make_async_remote_copy(
                    src_ref=tile_src.at[p, stage], dst_ref=landed.at[p, d - 1],
                    send_sem=ssem.at[p, d - 1], recv_sem=rsem.at[p, d - 1],
                    device_id={axis: lax.rem(idx + d, count)}, device_id_type=MESH,
                )
                for d in range(1, count)
            ]
            for copy in copies:
                copy.start()
            for d, copy in enumerate(copies):
                copy.wait_recv()
                value = value + landed[p, d]
            for copy in copies:
                copy.wait_send()
            return value

        grams = reduce_axis(grams, 0, "gx", ix, n_gx, ar_x, axs, axr)
        grams = reduce_axis(grams, 1, "gy", iy, n_gy, ar_y, ays, ayr)

        diff = grams - pltpu.roll(grams, lanes - probes, 1)
        upper = jnp.where(lane < 2 * probes, diff, pltpu.roll(grams, 2 * probes, 1))
        lower = jnp.where(lane < 2 * probes, pltpu.roll(diff, lanes - probes, 1), pltpu.roll(grams, probes, 1))
        size = 2 * probes
        both = [upper, lower]
        scale = [jnp.sum(jnp.where(lane == sub + h * probes, both[h], 0.0), axis=1, keepdims=True) for h in range(2)]
        for k in range(size):
            h, r = k // probes, k % probes
            row = both[h][r : r + 1, :]
            pivot = row[:, k : k + 1]
            inv = jnp.where(pivot > 1e-6 * scale[h][r : r + 1, :], 1.0 / pivot, 0.0)
            row = row * inv
            for q in range(2):
                updated = both[q] - both[q][:, k : k + 1] * row
                both[q] = jnp.where(sub == r, row, updated) if q == h else updated
        pick = (lane == sub + size).astype(jnp.float32)
        return lax.dot_general(
            pick, jnp.concatenate(both, axis=0), (((1,), (1,)), ((), ())),
            precision=HIGHEST, preferred_element_type=jnp.float32,
        )

    def mix(mixing, pairs):
        stacked = jnp.concatenate([jnp.concatenate(pair, axis=0) for pair in pairs], axis=1)
        mixed = lax.dot_general(
            mixing, stacked, (((1,), (0,)), ((), ())), precision=HIGHEST, preferred_element_type=jnp.float32
        )
        return [mixed[:, k * lanes : (k + 1) * lanes] for k in range(len(pairs))]

    mixing = solve(0)
    wm_edge = edge1[comps + 1]
    for c in range(2):
        k = c * layers + last
        inner = green[0, c, last]
        edge = unpack(merged3, k)
        pairs = [(xr3[0, k : k + 1, :] * bext[0, c, 0], ub[0, 0, k])]
        pairs += [(inner[i : i + 1, :] * bext[0, c, i + 1], ub[0, i + 1, k]) for i in range(rows)]
        pairs += [(xr3[1, k : k + 1, :] * bext[0, c, rows + 1], ub[0, rows + 1, k])]
        pairs += [(edge[i : i + 1, :] * bedge[0, c, i], uedge[c, i]) for i in range(rows)]
        mixed = mix(mixing, pairs)
        bext[1, c, 0] = mixed[0] * xr1[0, comps + 1 : comps + 2, :]
        bext[1, c, rows + 1] = mixed[rows + 1] * xr1[1, comps + 1 : comps + 2, :]
        for i in range(rows):
            bext[1, c, i + 1] = mixed[i + 1] * wm[i : i + 1, :]
            bedge[1, c, i] = mixed[rows + 2 + i] * wm_edge[i : i + 1, :]

    mixing = solve(1)
    results = []
    for c in range(2):
        inner = green[1, c, 0]
        results.append(mix(mixing, [
            (inner[i : i + 1, :] * bext[1, c, i + 1], ub[1, i + 1, c * layers]) for i in range(rows)
        ]))
    for i in range(rows):
        out_ref[:, i, :] = drive[0][i : i + 1, :] * results[0][i] + drive[1][i : i + 1, :] * results[1][i]


def body(sizes, velocity, thickness, log_friction, obs_weight, ice_mask, grounded, probes):
    layers, rows, lanes = velocity.shape[1:]
    count = probes.shape[0]
    comps = 2 * layers
    n_gx, n_gy = sizes
    rows1 = round_up(comps + 2, 8) + 2 * count
    rows2 = round_up(layers, 8)
    rows3 = round_up(2 * comps, 8)
    packs = rows // PAIR * count

    def vmem(*shape):
        return pltpu.VMEM(shape, jnp.float32)

    def borders(x_rows, y_rows):
        return [vmem(2, x_rows, lanes), vmem(2, x_rows, lanes), vmem(y_rows, lanes), vmem(2, y_rows, lanes)]

    sem = pltpu.SemaphoreType.DMA
    scratch = (
        borders(rows1, rows + count)
        + borders(rows2, rows)
        + borders(rows3, rows)
        + [vmem(2, packs, lanes), vmem(2, 2, packs, lanes), vmem(2, rows + 2, comps, count, lanes)]
        + [
            vmem(4, layers, rows, lanes), vmem(layers - 1, rows, lanes),
            vmem(2, layers - 1, rows, lanes), vmem(2, layers, rows, lanes),
            vmem(2, 2, layers, rows, lanes), vmem(2, 2, 4, layers, rows, lanes),
            vmem(2, 2, rows + 2, count, lanes), vmem(2, 2, rows, count, lanes), vmem(2, rows, count, lanes),
            vmem(2, rows, lanes), vmem(2, 2, count, lanes),
            vmem(2, n_gx - 1, count, lanes), vmem(2, n_gy - 1, count, lanes),
        ]
        + [sem((5, 4)), sem((5, 4)), sem((2, n_gx - 1)), sem((2, n_gx - 1)), sem((2, n_gy - 1)), sem((2, n_gy - 1))]
    )
    return pl.pallas_call(
        functools.partial(kernel, sizes),
        out_shape=jax.ShapeDtypeStruct(probes.shape, jnp.float32),
        in_specs=[pl.BlockSpec(memory_space=pltpu.VMEM)] * 7,
        out_specs=pl.BlockSpec(memory_space=pltpu.VMEM),
        scratch_shapes=scratch,
        compiler_params=pltpu.CompilerParams(collective_id=0, has_side_effects=True),
        name="hessian_probe",
    )(velocity, thickness, log_friction, obs_weight, ice_mask, grounded, probes)


def solution(mesh):
    sizes = (mesh.shape["gx"], mesh.shape["gy"])
    in_specs = (
        P(None, None, "gx", "gy"),
        P("gx", "gy"),
        P("gx", "gy"),
        P("gx", "gy"),
        P("gx", "gy"),
        P("gx", "gy"),
        P(None, "gx", "gy"),
    )
    out_specs = P(None, "gx", "gy")
    return jax.shard_map(
        functools.partial(body, sizes), mesh=mesh, in_specs=in_specs, out_specs=out_specs, check_vma=False
    )
```

profile of v0, /device:TPU:0, one launch (start us, length us, event | category | flops | bytes accessed | tf_op | source)
XLA Modules:
  0.0 47.0 jit_solution(13571137440414453197)
XLA Ops:
  0.0 45.6 %hessian_probe.1 = f32[8,8,128]{2,1,0:T(8,128)} custom-call(f32[2,11,8,128]{3,2,1,0:T(8,128)} %vel_ref.1, f32[8,128]{1,0:T(8,128)} %thick_ref.1, f32[8,128]{1,0:T(8,128)} %logf_ref.1, f32[8,128]{1,0:T(8,128)} %obs_ref.1, s32[8,128]{1,0:T(8,128)} %ice_ref.1, s32[8,128]{1,0:T(8,128)} %ground_ref.1, f32[8,8,128]{2,1,0:T(8,128)} %probes_ref.1), custom_call_target="tpu_custom_call" | custom-call | tf_op jit(solution)/shard_map/hessian_probe/pallas_call | solution.py:459
  45.6 1.4 %copy.9 = f32[8,8,128]{2,1,0:T(8,128)} copy(f32[8,8,128]{2,1,0:T(8,128)} %hessian_probe.1) | data formatting | bytes 65536
where the time goes:
time: 47.2 us; the launch traced here: 47 us
  Pallas kernels  45.6 us (97%)
  local copies, waits for them, and re-layouts  1.38 us (3%)
    pallas_call x1, Pallas kernels, body(): pl.pallas_call(functools.partial(kernel, sizes), out_shape=jax.ShapeDtype...  45.6 us
    unnamed x1, local copies, waits for them, and re-layouts  1.38 us

commit v1 on v0

--- a/solution.py
+++ b/solution.py
@@ -52,6 +52,7 @@
     sub_first = sub == 0
     sub_last = sub == rows - 1
 
+    sent = []
     barrier = pltpu.get_barrier_semaphore()
     for step in range(1, n_gx):
         pl.semaphore_signal(barrier, inc=1, device_id={"gx": lax.rem(ix + step, n_gx)}, device_id_type=MESH)
@@ -91,18 +92,27 @@
     def finish(transfers):
         for copy, _, has_dst, has_src in transfers:
             pl.when(has_src)(copy.wait_recv)
-        for copy, _, has_dst, has_src in transfers:
-            pl.when(has_dst)(copy.wait_send)
+        sent.extend((copy, has_dst) for copy, _, has_dst, _ in transfers)
 
     ex1 = exchange(0, (xs1.at[0], xs1.at[1]), (xr1.at[0], xr1.at[1]), ys1, (yr1.at[0], yr1.at[1]))
     ex2 = exchange(1, (xs2.at[0], xs2.at[1]), (xr2.at[0], xr2.at[1]), ys2, (yr2.at[0], yr2.at[1]))
     ex3 = exchange(2, (xs3.at[0], xs3.at[1]), (xr3.at[0], xr3.at[1]), ys3, (yr3.at[0], yr3.at[1]))
-    ex45 = [
-        exchange(
-            3 + p,
-            (ub.at[p, 1], ub.at[p, rows]), (ub.at[p, 0], ub.at[p, rows + 1]),
-            ys4.at[p], (yr4.at[p, 0], yr4.at[p, 1]),
-        )
+    pairs_of_rows = rows // PAIR
+    ex_rows = [
+        (transfer(3 + p, 0, ub.at[p, 1], ub.at[p, rows + 1]), transfer(3 + p, 1, ub.at[p, rows], ub.at[p, 0]))
+        for p in range(2)
+    ]
+    ex_packs = [
+        [
+            tuple(
+                transfer(
+                    3 + p + 2 * t, 2 + w, ys4.at[p, pl.ds(t * probes, probes)],
+                    yr4.at[p, 1 - w, pl.ds(t * probes, probes)],
+                )
+                for w in range(2)
+            )
+            for t in range(pairs_of_rows)
+        ]
         for p in range(2)
     ]
 
@@ -154,7 +164,7 @@
     ys1[0:rows, :] = pack(natural)
     ys1[rows:, :] = pack([bext[0, c, i + 1] for c in range(2) for i in range(rows)])
 
-    for ex in (ex1, ex2, ex3, ex45[0], ex45[1]):
+    for ex in [ex1, ex2, ex3] + ex_rows + ex_packs[0] + ex_packs[1]:
         clear(ex)
     pl.semaphore_wait(barrier, n_gx + n_gy - 2)
     start(ex1)
@@ -268,6 +278,15 @@
     def outer(acc, left, right):
         return tuple(acc[d] + left * ahead(right, d) for d in range(half + 1))
 
+    def place(grams, g, acc):
+        for d in range(half + 1):
+            total = jnp.broadcast_to(jnp.sum(acc[d], axis=1, keepdims=True), (probes, lanes))
+            grams = jnp.where(lane == g * probes + (sub + d) % probes, total, grams)
+            if 0 < d < half:
+                moved = pltpu.roll(total, d, 0)
+                grams = jnp.where(lane == g * probes + (sub + probes - d) % probes, moved, grams)
+        return grams
+
     def solve(p):
         src = 0 if p == 0 else last
         dst = last - src
@@ -308,16 +327,26 @@
                         if l == src:
                             acc_1 = outer(acc_1, b0, x)
                     acc_s = outer(acc_s, green[p, c, src, pl.ds(i, 1), :] * b0, b0)
-            ys4[p, pl.ds(pl.multiple_of(t * rows, rows), rows), :] = packed
+            ys4[p, pl.ds(t * probes, probes), :] = packed
             return acc_s, acc_1, acc_2
 
         none = (zero,) * (half + 1)
-        acc_s, acc_1, acc_2 = lax.fori_loop(0, rows // PAIR, first, (none, none, none))
-        start(ex45[p])
-        finish(ex45[p])
+        accs = (none, none, none)
+        order = [0, pairs_of_rows - 1] + list(range(1, pairs_of_rows - 1))
+        for n, t in enumerate(order):
+            accs = first(t, accs)
+            start(ex_packs[p][t])
+            if n == 1:
+                start(ex_rows[p])
+        grams = jnp.zeros((probes, lanes), jnp.float32)
+        for g in range(3):
+            grams = place(grams, g, accs[g])
+        for t in order:
+            finish(ex_packs[p][t])
+        finish(ex_rows[p])
 
         def second(t, acc_3):
-            at = pl.ds(pl.multiple_of(t * rows, rows), rows)
+            at = pl.ds(pl.multiple_of(t * probes, probes), probes)
             merged = merge(yr4[p, 0, at, :], yr4[p, 1, at, :])
             for ii in range(PAIR):
                 i = t * PAIR + ii
@@ -337,14 +366,7 @@
 
         acc_3 = lax.fori_loop(0, rows // PAIR, second, none)
 
-        grams = jnp.zeros((probes, lanes), jnp.float32)
-        for g, acc in enumerate((acc_s, acc_1, acc_2, acc_3)):
-            for d in range(half + 1):
-                total = jnp.broadcast_to(jnp.sum(acc[d], axis=1, keepdims=True), (probes, lanes))
-                grams = jnp.where(lane == g * probes + (sub + d) % probes, total, grams)
-                if 0 < d < half:
-                    moved = pltpu.roll(total, d, 0)
-                    grams = jnp.where(lane == g * probes + (sub + probes - d) % probes, moved, grams)
+        grams = place(grams, 3, acc_3)
 
         def reduce_axis(value, stage, axis, idx, count, landed, ssem, rsem):
             tile_src[p, stage] = value
@@ -361,8 +383,7 @@
             for d, copy in enumerate(copies):
                 copy.wait_recv()
                 value = value + landed[p, d]
-            for copy in copies:
-                copy.wait_send()
+            sent.extend((copy, None) for copy in copies)
             return value
 
         grams = reduce_axis(grams, 0, "gx", ix, n_gx, ar_x, axs, axr)
@@ -422,6 +443,11 @@
         ]))
     for i in range(rows):
         out_ref[:, i, :] = drive[0][i : i + 1, :] * results[0][i] + drive[1][i : i + 1, :] * results[1][i]
+    for copy, has_dst in sent:
+        if has_dst is None:
+            copy.wait_send()
+        else:
+            pl.when(has_dst)(copy.wait_send)
 
 
 def body(sizes, velocity, thickness, log_friction, obs_weight, ice_mask, grounded, probes):
@@ -454,7 +480,7 @@
             vmem(2, rows, lanes), vmem(2, 2, count, lanes),
             vmem(2, n_gx - 1, count, lanes), vmem(2, n_gy - 1, count, lanes),
         ]
-        + [sem((5, 4)), sem((5, 4)), sem((2, n_gx - 1)), sem((2, n_gx - 1)), sem((2, n_gy - 1)), sem((2, n_gy - 1))]
+        + [sem((3 + 2 * (rows // PAIR), 4)), sem((3 + 2 * (rows // PAIR), 4)), sem((2, n_gx - 1)), sem((2, n_gx - 1)), sem((2, n_gy - 1)), sem((2, n_gy - 1))]
     )
     return pl.pallas_call(
         functools.partial(kernel, sizes),

time: 47.2 us -> 47.1 us (level)
  no operation moved by 1% of the time
where the time goes in v1:
time: 47.1 us; the launch traced here: 46.9 us
  Pallas kernels  45.5 us (97%)
  local copies, waits for them, and re-layouts  1.38 us (3%)
    pallas_call x1, Pallas kernels, body(): pl.pallas_call(functools.partial(kernel, sizes), out_shape=jax.ShapeDtype...  45.5 us
    unnamed x1, local copies, waits for them, and re-layouts  1.38 us

profile of v1, /device:TPU:0, one launch (start us, length us, event | category | flops | bytes accessed | tf_op | source)
XLA Modules:
  0.0 46.9 jit_solution(16917054396832620249)
XLA Ops:
  0.0 45.5 %hessian_probe.1 = f32[8,8,128]{2,1,0:T(8,128)} custom-call(f32[2,11,8,128]{3,2,1,0:T(8,128)} %vel_ref.1, f32[8,128]{1,0:T(8,128)} %thick_ref.1, f32[8,128]{1,0:T(8,128)} %logf_ref.1, f32[8,128]{1,0:T(8,128)} %obs_ref.1, s32[8,128]{1,0:T(8,128)} %ice_ref.1, s32[8,128]{1,0:T(8,128)} %ground_ref.1, f32[8,8,128]{2,1,0:T(8,128)} %probes_ref.1), custom_call_target="tpu_custom_call" | custom-call | tf_op jit(solution)/shard_map/hessian_probe/pallas_call | solution.py:485
  45.5 1.4 %copy.9 = f32[8,8,128]{2,1,0:T(8,128)} copy(f32[8,8,128]{2,1,0:T(8,128)} %hessian_probe.1) | data formatting | bytes 65536
